TPU v7x, 512 devices: a whole 4x8x8 slice. The times are simulated.
512 devices in a mesh: tm: 64 (over z, x, core), band: 8 (over y).
Axes of the slice: x: 4, y: 8, z: 8, core: 2. Of those that a mesh axis runs over, the one named last changes fastest.
Arguments:
- query_input: bfloat16 [64, 40, 26, 1120], P('tm', 'band'), may hold values from -6 to 6
- key_input: bfloat16 [64, 40, 26, 1120], P('tm', 'band'), may hold values from -8 to 8
- value_input: bfloat16 [64, 40, 26, 1120], P('tm', 'band'), may hold values from -12 to 12
- cotangent: bfloat16 [64, 40, 26, 1120], P('tm', 'band'), may hold values from -6 to 6
- local_kernel_weight: float32 [3, 3, 1120], replicated, may hold values from -2 to 2
Outputs:
- mixed_out: bfloat16 [64, 40, 26, 1120], P('tm', 'band')
- query_grad: bfloat16 [64, 40, 26, 1120], P('tm', 'band')
- key_grad: bfloat16 [64, 40, 26, 1120], P('tm', 'band')
- value_grad: bfloat16 [64, 40, 26, 1120], P('tm', 'band')
- kernel_grad: float32 [3, 3, 1120], replicated
All inputs are finite; a program needn't handle non-finite values.
Results may differ from a plain program's by a relative error of at most 0.018.
Values may be sent and summed in bfloat16 or wider, within the bound.
No kernel may reach another device: no remote copies, remote signals or barrier semaphores. Data moves between devices by JAX's collectives and lax.ppermute only.
A program may use at most 128 MiB of HBM per device.

v0:
```python
import math
import jax
import jax.numpy as jnp
from jax import lax
from jax.sharding import PartitionSpec as P

HEADS = 35
HEAD_DIM = 32


def entering(shard, axis, combine, identity, reverse):
    devices, mine = (lax.axis_size(axis), lax.axis_index(axis))
    everything = jax.tree.map(lambda part: lax.all_gather(part, axis), shard)
    start = jax.tree.map(
        lambda part, zero: jnp.broadcast_to(jnp.asarray(zero, part.dtype), part.shape),
        shard,
        identity,
    )

    def step(k, before):
        at = devices - 1 - k if reverse else k
        reached = at > mine if reverse else at < mine
        new = combine(before, jax.tree.map(lambda part: part[at], everything))
        return jax.tree.map(lambda a, b: jnp.where(reached, a, b), new, before)

    return lax.fori_loop(0, devices, step, start)


def padded(cells, sides, width):
    for axis, dim in sides:
        count = lax.axis_size(axis)
        ends = count - 1
        head = lax.slice_in_dim(cells, 0, width, axis=dim)
        tail = lax.slice_in_dim(cells, cells.shape[dim] - width, cells.shape[dim], axis=dim)
        cells = jnp.concatenate(
            [
                lax.ppermute(tail, axis, [(i, (i + 1) % count) for i in range(ends)]),
                cells,
                lax.ppermute(head, axis, [((i + 1) % count, i) for i in range(ends)]),
            ],
            axis=dim,
        )
    return cells


def feature(x):
    return jnp.where(x > 0, x + 1.0, jnp.exp(jnp.minimum(x, 0.0)))


def slope(x):
    return jnp.where(x > 0, jnp.ones_like(x), jnp.exp(jnp.minimum(x, 0.0)))


def add_pair(earlier, later_term):
    return (earlier[0] + later_term[0], earlier[1] + later_term[1])


def frame_totals(terms, backward):
    frame = lax.psum(terms, "band")
    start = (jnp.zeros_like(frame[0]), jnp.zeros_like(frame[1]))
    before = entering(frame, "tm", add_pair, start, backward)
    return add_pair(before, frame)


def group_heads_count():
    chosen = 1
    for candidate in range(1, HEADS + 1):
        if HEADS % candidate == 0 and candidate * HEAD_DIM <= 256:
            chosen = candidate
    return chosen


def block_outer(left, right, group_count, group_heads, precise):
    count = left.shape[0]
    group_width = group_heads * HEAD_DIM
    left_groups = left.reshape(count, group_count, group_width)
    right_groups = right.reshape(count, group_count, group_width)
    if precise:
        whole = jnp.einsum(
            "tga,tgb->gab", left_groups, right_groups, precision=lax.Precision.HIGHEST
        )
    else:
        whole = jnp.einsum(
            "tga,tgb->gab", left_groups, right_groups, preferred_element_type=jnp.float32
        )
    whole = whole.reshape(group_count, group_heads, HEAD_DIM, group_heads, HEAD_DIM)
    same_head = jnp.eye(group_heads, dtype=jnp.float32)[None, :, None, :, None]
    return jnp.sum(whole * same_head, axis=3).reshape(HEADS, HEAD_DIM, HEAD_DIM)


def block_matrix(state, group_count, group_heads):
    group_width = group_heads * HEAD_DIM
    placed = state.reshape(group_count, group_heads, HEAD_DIM, 1, HEAD_DIM)
    same_head = jnp.eye(group_heads, dtype=jnp.float32)[None, :, None, :, None]
    return (placed * same_head).reshape(group_count, group_width, group_width)


def apply_blocks(rows, blocks, transposed):
    count = rows.shape[0]
    group_count, group_width = (blocks.shape[0], blocks.shape[1])
    grouped = rows.reshape(count, group_count, group_width)
    if transposed:
        result = jnp.einsum("tgb,gab->tga", grouped, blocks, precision=lax.Precision.HIGHEST)
    else:
        result = jnp.einsum("tga,gab->tgb", grouped, blocks, precision=lax.Precision.HIGHEST)
    return result.reshape(count, group_count * group_width)


def shards(query_input, key_input, value_input, cotangent, local_kernel_weight):
    high = lax.Precision.HIGHEST
    band_row_span, column_count, width = (
        query_input.shape[1],
        query_input.shape[2],
        query_input.shape[3],
    )
    count = band_row_span * column_count
    group_heads = group_heads_count()
    group_count = HEADS // group_heads
    indicator = (jnp.arange(width)[:, None] // HEAD_DIM == jnp.arange(HEADS)[None, :]).astype(
        jnp.float32
    )
    q_raw = query_input[0].reshape(count, width).astype(jnp.float32)
    k_raw = key_input[0].reshape(count, width).astype(jnp.float32)
    q_feat = feature(q_raw).astype(jnp.bfloat16)
    k_feat = feature(k_raw).astype(jnp.bfloat16)
    value_flat = value_input[0].reshape(count, width)
    own_state = block_outer(k_feat, value_flat, group_count, group_heads, False)
    own_norm = jnp.sum(k_feat, axis=0, dtype=jnp.float32).reshape(HEADS, HEAD_DIM)
    state, norm_vec = frame_totals((own_state, own_norm), False)
    q_wide = q_feat.astype(jnp.float32)
    state_blocks = block_matrix(state, group_count, group_heads)
    norm_flat = norm_vec.reshape(width)
    num = apply_blocks(q_wide, state_blocks, False)
    den = jnp.dot(q_wide * norm_flat, indicator, precision=high)
    den_wide = jnp.dot(den, indicator.T, precision=high)
    attn = num / den_wide
    stacked = jnp.stack([value_input[0], cotangent[0]])
    rimmed = padded(stacked, (("band", 1),), 1)
    padded_input = jnp.pad(rimmed, ((0, 0), (0, 0), (1, 1), (0, 0)))
    value_padded = padded_input[0]
    gpad = padded_input[1]
    complete_gradient = cotangent[0].astype(jnp.float32)
    local_output = jnp.zeros((band_row_span, column_count, width), jnp.float32)
    v_local = jnp.zeros((band_row_span, column_count, width), jnp.float32)
    kernel_row_slice = []
    for row_offset in range(3):
        for column_offset in range(3):
            local_output = (
                local_output
                + local_kernel_weight[row_offset, column_offset]
                * value_padded[
                    row_offset : row_offset + band_row_span,
                    column_offset : column_offset + column_count,
                ]
            )
            v_local = (
                v_local
                + local_kernel_weight[row_offset, column_offset]
                * gpad[
                    2 - row_offset : 2 - row_offset + band_row_span,
                    2 - column_offset : 2 - column_offset + column_count,
                ]
            )
            kernel_row_slice.append(
                jnp.sum(
                    complete_gradient
                    * value_padded[
                        row_offset : row_offset + band_row_span,
                        column_offset : column_offset + column_count,
                    ],
                    axis=(0, 1),
                )
            )
    mixed_out = (attn.reshape(band_row_span, column_count, width) + local_output).astype(
        jnp.bfloat16
    )[None]
    grad_flat = complete_gradient.reshape(count, width)
    scaled = grad_flat / den_wide
    den_grad = -jnp.dot(grad_flat * attn, indicator, precision=high) / den
    den_grad_wide = jnp.dot(den_grad, indicator.T, precision=high)
    back_state = block_outer(q_wide, scaled, group_count, group_heads, True)
    back_norm = jnp.sum(q_wide * den_grad_wide, axis=0).reshape(HEADS, HEAD_DIM)
    later_state, later_norm = frame_totals((back_state, back_norm), True)
    query_grad = apply_blocks(scaled, state_blocks, True) + den_grad_wide * norm_flat
    query_grad = (
        (query_grad * slope(q_raw))
        .reshape(band_row_span, column_count, width)
        .astype(jnp.bfloat16)[None]
    )
    later_blocks = block_matrix(later_state, group_count, group_heads)
    key_grad = apply_blocks(
        value_flat.astype(jnp.float32), later_blocks, True
    ) + later_norm.reshape(width)
    key_grad = (
        (key_grad * slope(k_raw))
        .reshape(band_row_span, column_count, width)
        .astype(jnp.bfloat16)[None]
    )
    value_grad = apply_blocks(k_feat.astype(jnp.float32), later_blocks, False)
    value_grad = (value_grad.reshape(band_row_span, column_count, width) + v_local).astype(
        jnp.bfloat16
    )[None]
    kernel_terms = jnp.stack(kernel_row_slice).reshape(3, 3, width)
    kernel_total = lax.psum(kernel_terms, ("tm", "band"))
    total_tokens = lax.axis_size("tm") * lax.axis_size("band") * count
    kernel_grad = kernel_total / math.sqrt(total_tokens)
    return (mixed_out, query_grad, key_grad, value_grad, kernel_grad)


def solution(mesh):
    placed = (
        P("tm", "band", None, None),
        P("tm", "band", None, None),
        P("tm", "band", None, None),
        P("tm", "band", None, None),
        P(),
    )
    return jax.shard_map(
        shards,
        mesh=mesh,
        in_specs=placed,
        out_specs=(
            P("tm", "band", None, None),
            P("tm", "band", None, None),
            P("tm", "band", None, None),
            P("tm", "band", None, None),
            P(),
        ),
        check_vma=False,
    )
```

profile of v0, /device:TPU:1, one launch (start us, length us, event | category | flops | bytes accessed | tf_op | source)
XLA Modules:
  0.0 863.7 jit_solution(13523367854085724787)
XLA Ops:
  10.0 2.6 reshape.180
  12.5 4.8 multiply_reduce_fusion.1
  17.4 79.9 %all-reduce.4.cloned.1.call-done = f32[35,32,32]{2,1,0:T(8,128)} async-done(((f32[35,32,32]{2,1,0:T(8,128)}), f32[35,32,32]{2,1,0:T(8,128)}) %all-reduce.4.cloned.1.call-update) | async-done | bytes 143376 | tf_op jit(solution)/shard_map/psum | solution.py:59
  97.5 22.3 %psum.36 = f32[35,32]{1,0:T(8,128)S(1)} all-reduce(f32[35,32]{1,0:T(8,128)S(1)} %reshape.182), channel_id=1, replica_groups=mesh['tm'=64,'band'=8] {'band'}, use_global_device_ids=true, to_apply=%region_3.4 | all-reduce | flops 1120 | bytes 8960 | tf_op jit(solution)/shard_map/psum | solution.py:59
  123.8 69.4 %all-gather.4 = f32[64,35,32]{1,2,0:T(8,128)} all-gather(f32[1,35,32]{1,2,0:T(8,128)S(1)} %copy.44), channel_id=3, replica_groups=mesh['tm'=64,'band'=8] {'tm'}, dimensions={0}, use_global_device_ids=true | all-gather | bytes 291200 | tf_op jit(solution)/shard_map/all_gather | solution.py:13
  193.2 69.6 %all-gather.9.cloned.1.call-done = f32[2240,32,32]{2,1,0:T(8,128)} async-done(((f32[35,32,32]{2,1,0:T(8,128)}), f32[2240,32,32]{2,1,0:T(8,128)}) %all-gather.9.cloned.1.call-update) | async-done | bytes 9175056 | tf_op jit(solution)/shard_map/all_gather | solution.py:13
  262.8 135.1 %while.34 = (s32[]{:T(128)}, f32[35,32,32]{2,1,0:T(8,128)S(1)}, f32[35,32]{1,0:T(8,128)S(1)}, s32[]{:T(128)}, f32[64,35,32,32]{3,2,1,0:T(8,128)}, /*index=5*/f32[64,35,32]{1,2,0:T(8,128)}, s32[]{:T(128)}, s32[]{:T(128)}) while((s32[]{:T(128)}, f32[35,32,32]{2,1,0:T(8,128)S(1)}, f32[35,32]{1,0:T(8,128)S(1)}, s32[]{:T(128)}, ...), condition=%wide.region_5.6_spmd.clone, body=%wide.region_4.5_spmd.clone.sunk | while | flops 110884 | bytes 461555 | solution.py:26
  398.0 2.4 mul.264
  400.4 3.6 mul.265
  405.9 2.4 reshape.183
  409.2 3.0 fusion.73
  415.7 3.9 reshape.187
  419.6 4.8 multiply_reduce_fusion
  424.4 70.0 %all-reduce.6.cloned.1.call-done = f32[35,32,32]{2,1,0:T(8,128)} async-done(((f32[35,32,32]{2,1,0:T(8,128)}), f32[35,32,32]{2,1,0:T(8,128)}) %all-reduce.6.cloned.1.call-update) | async-done | bytes 143376 | tf_op jit(solution)/shard_map/psum | solution.py:59
  494.6 3.2 collective-permute-start
  501.4 2.2 collective-permute-done.1
  506.2 107.4 %psum.39 = f32[3,3,1120]{2,1,0:T(4,128)S(1)} all-reduce(f32[3,3,1120]{2,1,0:T(4,128)S(1)} %reshape.191), channel_id=1, replica_groups=mesh['tm'=64,'band'=8] {'tm','band'}, use_global_device_ids=true, to_apply=%region_21.22 | all-reduce | flops 10080 | bytes 80640 | tf_op jit(solution)/shard_map/psum | solution.py:204
  614.3 3.1 convolution_bitcast_fusion.3
  620.9 2.2 fusion.4
  624.0 24.1 %psum.38 = f32[35,32]{1,0:T(8,128)S(1)} all-reduce(f32[35,32]{1,0:T(8,128)S(1)} %reshape.189), channel_id=1, replica_groups=mesh['tm'=64,'band'=8] {'band'}, use_global_device_ids=true, to_apply=%region_9.10 | all-reduce | flops 1120 | bytes 8960 | tf_op jit(solution)/shard_map/psum | solution.py:59
  649.0 58.1 %all-gather.5 = f32[64,35,32]{1,2,0:T(8,128)} all-gather(f32[1,35,32]{1,2,0:T(8,128)S(1)} %copy.52), channel_id=5, replica_groups=mesh['tm'=64,'band'=8] {'tm'}, dimensions={0}, use_global_device_ids=true | all-gather | bytes 291200 | tf_op jit(solution)/shard_map/all_gather | solution.py:13
  708.4 135.5 %while.35 = (s32[]{:T(128)}, f32[35,32,32]{2,1,0:T(8,128)S(1)}, f32[35,32]{1,0:T(8,128)S(1)}, s32[]{:T(128)}, f32[64,35,32,32]{3,2,1,0:T(8,128)}, /*index=5*/f32...) while((s32[]{:T(128)}, f32[35,32,32]{2,1,0:T(8,128)S(1)}, ...), condition=%wide.region_11.12_spmd.clone, body=%wide.region_10.11_spmd.clone.sunk | while | flops 110888 | bytes 461617 | solution.py:26
  844.0 2.4 mul.306
  846.4 3.6 mul.307
  (632 shorter events, 301.2 us)
Async XLA Ops:
  7.2 1.8 copy-start.17
  7.2 90.1 %all-reduce.4.cloned.1.call-start = ((), (), s32[]{:S(2)}) async-start(), calls=%async_computation | async-start | bytes 1146880 | tf_op jit(solution)/shard_map/psum | solution.py:59
  9.5 3.0 copy-start.7
  17.4 245.4 %all-gather.9.cloned.1.call-start = ((), (), s32[]{:S(2)}) async-start(), calls=%async_computation.2 | async-start | bytes 37273600 | tf_op jit(solution)/shard_map/all_gather | solution.py:13
  97.3 22.9 %copy-start.20 = (bf16[1,5,26,1120]{3,2,1,0:T(8,128)(2,1)S(1)}, bf16[1,5,26,1120]{3,2,1,0:T(8,128)(2,1)}, u32[]{:S(2)}) copy-start(bf16[1,5,26,1120]{3,2,1,0:T(8,128)(2,1)} %param.9) | copy-start | bytes 873604
  97.3 397.1 %all-reduce.6.cloned.1.call-start = ((), (), s32[]{:S(2)}) async-start(), calls=%async_computation.1 | async-start | bytes 1146880 | tf_op jit(solution)/shard_map/psum | solution.py:59
  122.7 285.6 %copy-start.1 = (f32[130,1120]{1,0:T(8,128)}, f32[130,1120]{1,0:T(8,128)S(1)}, u32[]{:S(2)}) copy-start(f32[130,1120]{1,0:T(8,128)S(1)} %reshape.192) | copy-start | bytes 1747204
  262.8 135.1 %copy-start.16 = (f32[35,32,32]{2,1,0:T(8,128)S(1)}, f32[35,32,32]{2,1,0:T(8,128)}, u32[]{:S(2)}) copy-start(f32[35,32,32]{2,1,0:T(8,128)} %all-reduce.4.cloned.1.call-done) | copy-start | bytes 430084
  400.4 3.6 copy-start.9
  412.2 1.5 copy-start.10
  413.7 5.8 copy-start
  424.4 70.1 %copy-start.18 = (bf16[1,5,26,1120]{3,2,1,0:T(8,128)(2,1)S(1)}, bf16[1,5,26,1120]{3,2,1,0:T(8,128)(2,1)}, u32[]{:S(2)}) copy-start(bf16[1,5,26,1120]{3,2,1,0:T(8,128)(2,1)} %param.11) | copy-start | bytes 873604
  424.4 284.0 %all-gather.11.cloned.1.call-start = ((), (), s32[]{:S(2)}) async-start(), calls=%async_computation.3 | async-start | bytes 37273600 | tf_op jit(solution)/shard_map/all_gather | solution.py:13
  494.5 3.2 copy-start.12
  494.5 6.8 copy-start.21
  494.6 6.9 collective-permute-start
  497.8 5.9 collective-permute-start.1
  618.8 4.3 copy-start.2
  620.9 2.2 copy-start.13
  620.9 2.2 copy-start.14
  623.9 83.1 %copy-start.4 = (f32[5,26,1120]{2,1,0:T(8,128)S(1)}, f32[5,26,1120]{2,1,0:T(8,128)}, u32[]{:S(2)}) copy-start(f32[5,26,1120]{2,1,0:T(8,128)} %reshape.184) | copy-start | bytes 1747204
  708.4 135.5 %copy-start.15 = (f32[35,32,32]{2,1,0:T(8,128)S(1)}, f32[35,32,32]{2,1,0:T(8,128)}, u32[]{:S(2)}) copy-start(f32[35,32,32]{2,1,0:T(8,128)} %all-reduce.6.cloned.1.call-done) | copy-start | bytes 430084
  846.4 3.6 copy-start.6
  854.8 1.4 copy-start.19
  (4 other events, 4.5 us)
Sparse Core Ops, SparseCore 0:
  17.5 79.7 all-reduce.3
  100.6 162.1 all-gather.8
  424.5 69.8 all-reduce.5
  497.6 161.7 all-gather.10
where the time goes:
time: 877 us; the launch traced here: 864 us
  blocking collectives  281 us (32%)
  waiting for transfers between devices  222 us (25%)
  other arithmetic  182 us (21%)
  local copies, waits for them, and re-layouts  141 us (16%)
  matrix products  15.3 us (2%)
  between operations  14.3 us (2%)
    select_n x256, other arithmetic, step(): return jax.tree.map(lambda a, b: jnp.where(reached, a, b), new, before)  163 us
    psum x2, waiting for transfers between devices, frame_totals(): frame = lax.psum(terms, 'band')  150 us
    all_gather x2, blocking collectives, entering(): everything = jax.tree.map(lambda part: lax.all_gather(part, axis), shard)  127 us
    psum x1, blocking collectives, shards(): kernel_total = lax.psum(kernel_terms, ('tm', 'band'))  107 us
    dynamic_slice x256, local copies, waits for them, and re-layouts, step(): new = combine(before, jax.tree.map(lambda part: part[at], everything))  104 us
    all_gather x2, waiting for transfers between devices, entering(): everything = jax.tree.map(lambda part: lax.all_gather(part, axis), shard)  69.6 us
    psum x2, blocking collectives, frame_totals(): frame = lax.psum(terms, 'band')  46.4 us
  transfers between devices with their start and end apart: 6, of which 4 were waited for; matrix products, arithmetic and copies ran while one was open for 2% of the time, Pallas kernels for 0%

commit v1 on v0

--- a/solution.py
+++ b/solution.py
@@ -1,11 +1,22 @@
+import functools
 import math
 import jax
 import jax.numpy as jnp
 from jax import lax
 from jax.sharding import PartitionSpec as P
+from jax.lax import psum
 
 HEADS = 35
 HEAD_DIM = 32
+
+
+def see_the_state(content, dev_axis, along_axis):
+    for rr in (dev_axis, along_axis):
+        content = psum(content, rr)
+    return content
+
+
+unite_the_spans = functools.partial(see_the_state, dev_axis="band", along_axis="tm")
 
 
 def entering(shard, axis, combine, identity, reverse):
@@ -201,7 +212,7 @@
         jnp.bfloat16
     )[None]
     kernel_terms = jnp.stack(kernel_row_slice).reshape(3, 3, width)
-    kernel_total = lax.psum(kernel_terms, ("tm", "band"))
+    kernel_total = unite_the_spans(kernel_terms)
     total_tokens = lax.axis_size("tm") * lax.axis_size("band") * count
     kernel_grad = kernel_total / math.sqrt(total_tokens)
     return (mixed_out, query_grad, key_grad, value_grad, kernel_grad)

time: 877 us -> 1030 us (1.17)
  blocking collectives: 281 us -> 432 us
    psum x1, blocking collectives: 107 us -> 255 us  [see_the_state(): content = psum(content, rr)]
  transfers between devices with their start and end apart: 6 -> 6, of which waited for: 4 -> 3; matrix products, arithmetic and copies ran while one was open for 2% -> 2% of each run, Pallas kernels for 0% -> 0%
where the time goes in v1:
time: 1030 us; the launch traced here: 1020 us
  blocking collectives  432 us (42%)
  waiting for transfers between devices  219 us (21%)
  other arithmetic  181 us (18%)
  local copies, waits for them, and re-layouts  145 us (14%)
  matrix products  15 us (1%)
  between operations  14.3 us (1%)
    psum x1, blocking collectives, see_the_state(): content = psum(content, rr)  255 us
    select_n x256, other arithmetic, step(): return jax.tree.map(lambda a, b: jnp.where(reached, a, b), new, before)  163 us
    psum x2, waiting for transfers between devices, frame_totals(): frame = lax.psum(terms, 'band')  150 us
    all_gather x2, blocking collectives, entering(): everything = jax.tree.map(lambda part: lax.all_gather(part, axis), shard)  128 us
    dynamic_slice x256, local copies, waits for them, and re-layouts, step(): new = combine(before, jax.tree.map(lambda part: part[at], everything))  104 us
    all_gather x2, waiting for transfers between devices, entering(): everything = jax.tree.map(lambda part: lax.all_gather(part, axis), shard)  69.6 us
    psum x2, blocking collectives, frame_totals(): frame = lax.psum(terms, 'band')  48.4 us
  transfers between devices with their start and end apart: 6, of which 3 were waited for; matrix products, arithmetic and copies ran while one was open for 2% of the time, Pallas kernels for 0%

profile of v1, /device:TPU:1, one launch (start us, length us, event | category | flops | bytes accessed | tf_op | source)
XLA Modules:
  0.0 1015.5 jit_solution(7642302817372191673)
XLA Ops:
  10.0 2.6 reshape.180
  12.5 4.8 multiply_reduce_fusion.1
  17.4 79.9 %all-reduce.5.cloned.1.call-done = f32[35,32,32]{2,1,0:T(8,128)} async-done(((f32[35,32,32]{2,1,0:T(8,128)}), f32[35,32,32]{2,1,0:T(8,128)}) %all-reduce.5.cloned.1.call-update) | async-done | bytes 143376 | tf_op jit(solution)/shard_map/psum | solution.py:70
  98.4 22.5 %psum.43 = f32[35,32]{1,0:T(8,128)S(1)} all-reduce(f32[35,32]{1,0:T(8,128)S(1)} %reshape.182), channel_id=1, replica_groups=mesh['tm'=64,'band'=8] {'band'}, use_global_device_ids=true, to_apply=%region_3.4 | all-reduce | flops 1120 | bytes 8960 | tf_op jit(solution)/shard_map/psum | solution.py:70
  123.8 69.4 %all-gather.4 = f32[64,35,32]{1,2,0:T(8,128)} all-gather(f32[1,35,32]{1,2,0:T(8,128)S(1)} %copy.44), channel_id=3, replica_groups=mesh['tm'=64,'band'=8] {'tm'}, dimensions={0}, use_global_device_ids=true | all-gather | bytes 291200 | tf_op jit(solution)/shard_map/all_gather | solution.py:24
  193.2 69.6 %all-gather.9.cloned.1.call-done = f32[2240,32,32]{2,1,0:T(8,128)} async-done(((f32[35,32,32]{2,1,0:T(8,128)}), f32[2240,32,32]{2,1,0:T(8,128)}) %all-gather.9.cloned.1.call-update) | async-done | bytes 9175056 | tf_op jit(solution)/shard_map/all_gather | solution.py:24
  262.7 135.1 %while.34 = (s32[]{:T(128)}, f32[35,32,32]{2,1,0:T(8,128)S(1)}, f32[35,32]{1,0:T(8,128)S(1)}, s32[]{:T(128)}, f32[64,35,32,32]{3,2,1,0:T(8,128)}, /*index=5*/f32[64,35,32]{1,2,0:T(8,128)}, s32[]{:T(128)}, s32[]{:T(128)}) while((s32[]{:T(128)}, f32[35,32,32]{2,1,0:T(8,128)S(1)}, f32[35,32]{1,0:T(8,128)S(1)}, s32[]{:T(128)}, ...), condition=%wide.region_5.6_spmd.clone, body=%wide.region_4.5_spmd.clone.sunk | while | flops 110884 | bytes 461563 | solution.py:37
  397.9 2.4 mul.264
  400.3 3.6 mul.265
  405.8 2.4 reshape.183
  409.1 3.0 fusion.73
  415.7 3.9 reshape.187
  419.5 4.8 multiply_reduce_fusion
  424.4 70.0 %all-reduce.7.cloned.1.call-done = f32[35,32,32]{2,1,0:T(8,128)} async-done(((f32[35,32,32]{2,1,0:T(8,128)}), f32[35,32,32]{2,1,0:T(8,128)}) %all-reduce.7.cloned.1.call-update) | async-done | bytes 143376 | tf_op jit(solution)/shard_map/psum | solution.py:70
  496.7 4.2 collective-permute-start
  507.7 2.8 convolution_bitcast_fusion.3
  511.8 2.5 reshape.186
  514.3 2.2 fusion.4
  518.2 26.0 %all-reduce.1 = (f32[35,32]{1,0:T(8,128)S(1)}, f32[3,3,1120]{2,1,0:T(4,128)S(1)}) all-reduce(f32[35,32]{1,0:T(8,128)S(1)} %reshape.189, f32[3,3,1120]{2,1,0:T(4,128)S(1)} %reshape.191), channel_id=1, replica_groups=mesh['tm'=64,'band'=8] {'band'}, use_global_device_ids=true, to_apply=%region_9.10 | all-reduce | flops 11200 | bytes 89600 | tf_op jit(solution)/shard_map/psum | solution.py:70
  544.2 255.4 %psum.47 = f32[3,3,1120]{2,1,0:T(4,128)S(1)} all-reduce(f32[3,3,1120]{2,1,0:T(4,128)S(1)} %get-tuple-element.371), channel_id=1, replica_groups=mesh['tm'=64,'band'=8] {'tm'}, use_global_device_ids=true, to_apply=%region_22.23 | all-reduce | flops 10080 | bytes 80640 | tf_op jit(solution)/shard_map/psum | solution.py:15
  799.6 58.4 %all-gather.5 = f32[64,35,32]{1,2,0:T(8,128)} all-gather(f32[1,35,32]{1,2,0:T(8,128)S(1)} %copy.52), channel_id=5, replica_groups=mesh['tm'=64,'band'=8] {'tm'}, dimensions={0}, use_global_device_ids=true | all-gather | bytes 291200 | tf_op jit(solution)/shard_map/all_gather | solution.py:24
  860.0 135.4 %while.35 = (s32[]{:T(128)}, f32[35,32,32]{2,1,0:T(8,128)S(1)}, f32[35,32]{1,0:T(8,128)S(1)}, s32[]{:T(128)}, f32[64,35,32,32]{3,2,1,0:T(8,128)}, /*index=5*/f32...) while((s32[]{:T(128)}, f32[35,32,32]{2,1,0:T(8,128)S(1)}, ...), condition=%wide.region_11.12_spmd.clone, body=%wide.region_10.11_spmd.clone.sunk | while | flops 110888 | bytes 461625 | solution.py:37
  995.5 2.4 mul.306
  997.9 3.6 mul.307
  (632 shorter events, 301.8 us)
Async XLA Ops:
  7.2 1.6 copy-start.18
  7.2 90.1 %all-reduce.5.cloned.1.call-start = ((), (), s32[]{:S(2)}) async-start(), calls=%async_computation | async-start | bytes 1146880 | tf_op jit(solution)/shard_map/psum | solution.py:70
  8.7 1.2 copy-start.5
  9.5 3.0 copy-start.7
  17.3 80.1 %copy-start.3 = (bf16[1,5,26,1120]{3,2,1,0:T(8,128)(2,1)S(1)}, bf16[1,5,26,1120]{3,2,1,0:T(8,128)(2,1)}, u32[]{:S(2)}) copy-start(bf16[1,5,26,1120]{3,2,1,0:T(8,128)(2,1)} %param.12) | copy-start | bytes 873604
  17.3 245.4 %all-gather.9.cloned.1.call-start = ((), (), s32[]{:S(2)}) async-start(), calls=%async_computation.2 | async-start | bytes 37273600 | tf_op jit(solution)/shard_map/all_gather | solution.py:24
  97.3 397.1 %all-reduce.7.cloned.1.call-start = ((), (), s32[]{:S(2)}) async-start(), calls=%async_computation.1 | async-start | bytes 1146880 | tf_op jit(solution)/shard_map/psum | solution.py:70
  98.3 23.0 %copy-start.20 = (bf16[1,5,26,1120]{3,2,1,0:T(8,128)(2,1)S(1)}, bf16[1,5,26,1120]{3,2,1,0:T(8,128)(2,1)}, u32[]{:S(2)}) copy-start(bf16[1,5,26,1120]{3,2,1,0:T(8,128)(2,1)} %param.9) | copy-start | bytes 873604
  123.7 284.6 %copy-start.1 = (f32[130,1120]{1,0:T(8,128)}, f32[130,1120]{1,0:T(8,128)S(1)}, u32[]{:S(2)}) copy-start(f32[130,1120]{1,0:T(8,128)S(1)} %reshape.192) | copy-start | bytes 1747204
  262.7 135.1 %copy-start.16 = (f32[35,32,32]{2,1,0:T(8,128)S(1)}, f32[35,32,32]{2,1,0:T(8,128)}, u32[]{:S(2)}) copy-start(f32[35,32,32]{2,1,0:T(8,128)} %all-reduce.5.cloned.1.call-done) | copy-start | bytes 430084
  400.3 3.6 copy-start.9
  412.2 1.5 copy-start.10
  413.7 5.8 copy-start
  424.3 70.1 %copy-start.17 = (bf16[1,5,26,1120]{3,2,1,0:T(8,128)(2,1)S(1)}, bf16[1,5,26,1120]{3,2,1,0:T(8,128)(2,1)}, u32[]{:S(2)}) copy-start(bf16[1,5,26,1120]{3,2,1,0:T(8,128)(2,1)} %param.11) | copy-start | bytes 873604
  424.4 435.6 %all-gather.11.cloned.1.call-start = ((), (), s32[]{:S(2)}) async-start(), calls=%async_computation.3 | async-start | bytes 37273600 | tf_op jit(solution)/shard_map/all_gather | solution.py:24
  495.4 7.6 copy-start.21
  495.4 7.7 collective-permute-start.1
  496.7 6.4 collective-permute-start
  511.8 4.6 copy-start.2
  514.3 2.2 copy-start.13
  514.3 2.2 copy-start.14
  517.2 341.4 %copy-start.4 = (f32[5,26,1120]{2,1,0:T(8,128)S(1)}, f32[5,26,1120]{2,1,0:T(8,128)}, u32[]{:S(2)}) copy-start(f32[5,26,1120]{2,1,0:T(8,128)} %reshape.184) | copy-start | bytes 1747204
  860.0 135.4 %copy-start.15 = (f32[35,32,32]{2,1,0:T(8,128)S(1)}, f32[35,32,32]{2,1,0:T(8,128)}, u32[]{:S(2)}) copy-start(f32[35,32,32]{2,1,0:T(8,128)} %all-reduce.7.cloned.1.call-done) | copy-start | bytes 430084
  997.9 3.6 copy-start.6
  (4 other events, 4.1 us)
Sparse Core Ops, SparseCore 0:
  17.5 79.7 all-reduce.4
  100.6 162.1 all-gather.8
  424.5 69.8 all-reduce.6
  497.5 161.2 all-gather.10
